TPU v7x, 256 devices: a whole 4x4x8 slice. The times are simulated.
256 devices in a mesh: tx: 4 (over z_lo, core), img: 64 (over y, z_hi, x).
Axes of the slice: x: 4, y: 4, z: 8 (z_hi: 4, z_lo: 2; z = z_hi * 2 + z_lo), core: 2. Of those that a mesh axis runs over, the one named last changes fastest.
Arguments:
- encoded: bfloat16 [1024, 1024, 512], P('tx', 'img'), may hold values from -6 to 6
- signs: int32 [1024, 64], replicated, may hold values from -1 to 1, as said below
- tx_block: int32 [64, 16384], P('tx'), may hold values from 0 to 1
- rx_block: int32 [1024, 16384], P(None, 'img'), may hold values from 0 to 2
- apodization: int32 [1024, 16384], P(None, 'img'), may hold values 0 or 1
Outputs:
- image: float32 [16384, 128], P('img', 'tx')
Inputs may be any that keep to these rules, and one draw needn't show every extreme that they name: `signs`: every entry is 1 or -1. The columns are 64 distinct columns of the Sylvester Hadamard matrix of order 1024, every row multiplied by its own sign, so that two different columns are orthogonal.
All inputs are finite; a program needn't handle non-finite values. No bound on the sum of `apodization` on one device may be relied on, other than what follows from the above.
Results may differ from a plain program's by a relative error of at most 0.0029.
Values may be sent and summed in bfloat16 or wider, within the bound.
A program may use at most 192 MiB of HBM per device.

v0:
```python
import math

import jax
import jax.numpy as jnp
from jax import lax
from jax.sharding import PartitionSpec as P

E = 1024
K = 64
R = 1024
L = 128


def weights_for(rx_rows, mask_rows, tx_rows, block_count):
    total_block = tx_rows.T[:, :, None] + rx_rows.T[:, None, :]
    levels = jnp.arange(block_count, dtype=jnp.int32)
    chosen = total_block[..., None] == levels
    weight = jnp.where(
        chosen, mask_rows.T[:, None, :, None].astype(jnp.bfloat16), jnp.zeros((), jnp.bfloat16)
    )
    return weight.reshape(weight.shape[0], -1)


def on_device(encoded, signs, tx_block, rx_block, apodization):
    events_here, receivers_here, sample_count = encoded.shape
    transmits_here = tx_block.shape[0]
    lines_here = rx_block.shape[1]
    block_count = sample_count // L
    tx_index = lax.axis_index("tx")
    img_index = lax.axis_index("img")
    sign_cols = lax.dynamic_slice_in_dim(
        signs, tx_index * transmits_here, transmits_here, 1
    ).astype(jnp.bfloat16)
    piece = lax.all_gather(encoded, "tx", axis=0, tiled=True)
    flat_piece = piece.reshape(piece.shape[0], -1)
    summed = lax.dot_general(
        sign_cols, flat_piece, (((0,), (0,)), ((), ())), preferred_element_type=jnp.float32
    )
    decoded = (
        (summed * (1.0 / E))
        .astype(jnp.bfloat16)
        .reshape(transmits_here, receivers_here, sample_count)
    )
    own_tx = lax.dynamic_slice_in_dim(tx_block, img_index * lines_here, lines_here, 1)
    weight = weights_for(rx_block, apodization, own_tx, block_count)
    image = jnp.dot(
        weight,
        lax.all_gather(decoded, "img", axis=1, tiled=True).reshape(-1, L),
        preferred_element_type=jnp.float32,
    )
    scale = math.sqrt(E / (K * R))
    return lax.psum_scatter(image * scale, "tx", scatter_dimension=1, tiled=True)


def solution(mesh):
    placed = (P("tx", "img", None), P(), P("tx", None), P(None, "img"), P(None, "img"))
    return jax.shard_map(
        on_device, mesh=mesh, in_specs=placed, out_specs=P("img", "tx"), check_vma=False
    )
```

profile of v0, /device:TPU:2, one launch (start us, length us, event | category | flops | bytes accessed | tf_op | source)
XLA Modules:
  0.0 435.4 jit_solution(3269793722373958199)
XLA Ops:
  6.5 0.0 copy-start
  6.5 0.0 all-gather.3.cloned.1.call-start
  6.5 0.7 all-gather.3.cloned.1.call-update
  7.3 0.0 all-gather.5.cloned.1.call-start
  7.3 156.8 %all-gather.3.cloned.1.call-done = bf16[1024,16,512]{2,1,0:T(8,128)(2,1)} async-done(((bf16[256,16,512]{2,1,0:T(8,128)(2,1)}), bf16[1024,16,512]{2,1,0:T(8,128)(2,1)}) %all-gather.3.cloned.1.call-update) | async-done | bytes 16777232 | tf_op jit(solution)/shard_map/all_gather | solution.py:34
  164.1 15.8 %copy.9 = bf16[128,8,16,512]{3,1,2,0:T(8,128)(2,1)S(1)} copy(bf16[128,8,16,512]{3,2,1,0:T(8,128)(2,1)} %bitcast.15) | data formatting | bytes 33554432
  179.9 0.0 copy-start.3
  179.9 0.0 copy-start.2
  180.0 3.3 fusion.1
  183.2 0.8 copy.10
  184.0 0.0 all-gather.5.cloned.1.call-update
  184.1 0.0 reduce-scatter.2.cloned.1.call-start
  184.1 0.0 copy-done
  184.1 0.0 copy-done.3
  184.1 0.1 convert_bitcast_fusion
  184.2 0.0 copy-done.2
  184.2 7.4 %broadcast_add_fusion = s32[256,16,1024]{0,2,1:T(8,128)} fusion(s32[256,1024]{0,1:T(8,128)S(1)} %bitcast.17, s32[256,16]{0,1:T(8,128)S(1)} %dynamic-slice_bitcast_fusion), kind=kLoop, calls=%fused_computation.4 | loop fusion | flops 4194304 | bytes 17842176 | tf_op jit(solution)/shard_map/add | solution.py:15
  191.6 21.2 %fusion = bf16[256,16,1024,4]{0,3,2,1:T(4,128)(2,1)} fusion(s32[256,16,1024]{0,2,1:T(8,128)} %broadcast_add_fusion, bf16[256,1024]{0,1:T(8,128)(2,1)S(1)} %convert_bitcast_fusion), kind=kLoop, calls=%fused_computation.1 | loop fusion | flops 33554432 | bytes 50855936 | tf_op jit(solution)/shard_map/jit(_where)/select_n | solution.py:18
  212.8 46.2 %select_n.22 = bf16[256,65536]{0,1:T(8,128)(2,1)} reshape(bf16[256,16,1024,4]{0,3,2,1:T(4,128)(2,1)} %fusion) | data formatting | bytes 67108864 | tf_op jit(solution)/shard_map/jit(_where)/select_n | solution.py:18
  259.1 89.3 %all-gather.5.cloned.1.call-done = bf16[16,1024,512]{2,1,0:T(8,128)(2,1)} async-done(((bf16[16,16,512]{2,1,0:T(8,128)(2,1)}), bf16[16,1024,512]{2,1,0:T(8,128)(2,1)}) %all-gather.5.cloned.1.call-update) | async-done | bytes 16777232 | tf_op jit(solution)/shard_map/all_gather | solution.py:48
  348.4 26.6 %reshape.55 = bf16[65536,128]{1,0:T(8,128)(2,1)} reshape(bf16[16,1024,512]{2,1,0:T(8,128)(2,1)} %all-gather.5.cloned.1.call-done) | data formatting | bytes 33554432 | tf_op jit(solution)/shard_map/reshape | solution.py:48
  375.0 0.0 copy-start.1
  375.0 18.7 %convolution_multiply_fusion.1 = f32[256,128]{0,1:T(8,128)} fusion(bf16[256,65536]{0,1:T(8,128)(2,1)} %select_n.22, bf16[65536,128]{1,0:T(8,128)(2,1)} %reshape.55), kind=kOutput, calls=%fused_computation.5 | convolution fusion | flops 4295000064 | bytes 50462720 | tf_op jit(solution)/shard_map/dot_general | solution.py:46
  393.8 0.0 reduce-scatter.2.cloned.1.call-update
  393.8 35.0 %reduce-scatter.2.cloned.1.call-done = f32[256,32]{0,1:T(8,128)} async-done(((f32[256,128]{0,1:T(8,128)}), f32[256,32]{0,1:T(8,128)}) %reduce-scatter.2.cloned.1.call-update) | async-done | bytes 32784 | tf_op jit(solution)/shard_map/reduce_scatter | solution.py:52
  428.8 0.0 copy-done.1
  (1 shorter events, 0.0 us)
Async XLA Ops:
  6.5 177.6 %copy-start = (s32[16,16384]{1,0:T(8,128)S(1)}, s32[16,16384]{1,0:T(8,128)}, u32[]{:S(2)}) copy-start(s32[16,16384]{1,0:T(8,128)} %param.7) | copy-start | bytes 3145732
  6.5 157.5 %all-gather.3.cloned.1.call-start = ((), (), s32[]{:S(2)}) async-start(), calls=%async_computation.1 | async-start | bytes 20971520 | tf_op jit(solution)/shard_map/all_gather | solution.py:34
  7.3 341.1 %all-gather.5.cloned.1.call-start = ((), (), s32[]{:S(2)}) async-start(), calls=%async_computation.2 | async-start | bytes 17039360 | tf_op jit(solution)/shard_map/all_gather | solution.py:48
  179.9 4.2 copy-start.3
  179.9 4.3 copy-start.2
  184.1 244.8 %reduce-scatter.2.cloned.1.call-start = ((), (), s32[]{:S(2)}) async-start(), calls=%async_computation.3 | async-start | bytes 163840 | tf_op jit(solution)/shard_map/reduce_scatter | solution.py:52
  375.0 53.8 %copy-start.1 = (s32[16,16384]{1,0:T(8,128)S(1)}, s32[16,16384]{1,0:T(8,128)}, u32[]{:S(2)}) copy-start(s32[16,16384]{1,0:T(8,128)} %param.7) | copy-start | bytes 3145732
Sparse Core Ops, SparseCore 0:
  9.1 154.8 all-gather.2
  184.2 164.1 all-gather.4
  393.9 34.8 reduce-scatter.1
where the time goes:
time: 439 us; the launch traced here: 435 us
  waiting for transfers between devices  282 us (64%)
  local copies, waits for them, and re-layouts  89.6 us (20%)
  other arithmetic  28.7 us (7%)
  matrix products  22 us (5%)
  between operations  13.2 us (3%)
    all_gather x1, waiting for transfers between devices, on_device(): piece = lax.all_gather(encoded, 'tx', axis=0, tiled=True)  157 us
    all_gather x1, waiting for transfers between devices, on_device(): lax.all_gather(decoded, 'img', axis=1, tiled=True).reshape(-1, L)  89.3 us
    select_n x1, local copies, waits for them, and re-layouts, weights_for(): jnp.where(chosen, mask_rows.T[:, None, :, None].astype(jnp.bfloat16), jnp...  46.2 us
    reduce_scatter x1, waiting for transfers between devices, on_device(): lax.psum_scatter(image * scale, 'tx', scatter_dimension=1, tiled=True)  35 us
    reshape x1, local copies, waits for them, and re-layouts, on_device(): lax.all_gather(decoded, 'img', axis=1, tiled=True).reshape(-1, L)  26.6 us
    select_n x1, other arithmetic, weights_for(): jnp.where(chosen, mask_rows.T[:, None, :, None].astype(jnp.bfloat16), jnp...  21.2 us
    dot_general x1, matrix products, on_device(): jnp.dot(weight, lax.all_gather(decoded, 'img', axis=1, tiled=True).reshap...  18.7 us
    unnamed x10, local copies, waits for them, and re-layouts  16.7 us
  transfers between devices with their start and end apart: 3, of which 3 were waited for; matrix products, arithmetic and copies ran while one was open for 17% of the time, Pallas kernels for 0%

commit v1 on v0

v1 whole, which is shorter than its diff:
```python
import jax
import jax.numpy as jnp
from jax import lax
from jax.experimental import pallas as pl
from jax.experimental.pallas import tpu as pltpu
from jax.sharding import PartitionSpec as P

MESH = pl.DeviceIdType.MESH
F32 = jnp.float32
BF16 = jnp.bfloat16
LG = 256


def kernel(
    enc_hbm, signs_hbm, tx_hbm, rx_hbm, apo_hbm, out_ref,
    encb, encf, sg, part, rb, zs, zb, da, dt, sh, rxi, rxs, rxa, txi,
    delta, keep, send, ib, ys, yb, zss, zrb,
    ld_enc, ld_rx, ld_sg, ld_tx,
    rx_s, rx_r, fw_s, fw_r, sw_s, sw_r, ze_s, ze_r, xg_s, xg_r,
    ci_s, ci_r, y_s, y_r, z_s, z_r,
):
    tx = lax.axis_index("tx")
    img = lax.axis_index("img")
    zl = tx // 2
    co = tx % 2
    y = img // 16
    zh = (img // 4) % 4
    x = img % 4
    z = zh * 2 + zl
    g = y * 4 + zh

    def dev(xx, yy, zz, cc):
        return {"tx": (zz % 2) * 2 + cc, "img": (yy * 4 + zz // 2) * 4 + xx}

    partner = dev(x, y, z, 1 - co)
    mate = dev(x, y, zh * 2 + (1 - zl), co)
    xr = (x + 1) % 4
    xl = (x + 3) % 4
    right = dev(xr, y, z, co)
    left = dev(xl, y, z, co)

    def rcopy(src, dst, ss, rs, to):
        return pltpu.make_async_remote_copy(
            src_ref=src, dst_ref=dst, send_sem=ss, recv_sem=rs,
            device_id=to, device_id_type=MESH,
        )

    def enc_load(i):
        return pltpu.make_async_copy(
            enc_hbm.at[pl.ds(64 * i, 64)], encb.at[pl.ds(64 * i, 64)], ld_enc.at[i]
        )

    l_rx = pltpu.make_async_copy(rx_hbm, rxi.at[0], ld_rx.at[0])
    l_ap = pltpu.make_async_copy(apo_hbm, rxi.at[1], ld_rx.at[1])
    l_sg = pltpu.make_async_copy(
        signs_hbm.at[pl.ds(pl.multiple_of(256 * tx, 256), 256)], sg, ld_sg
    )
    l_rx.start()
    l_ap.start()
    l_sg.start()
    for i in range(4):
        enc_load(i).start()

    def tx_load(i):
        return pltpu.make_async_copy(
            tx_hbm.at[:, pl.ds(pl.multiple_of(LG * (4 * i + x), LG), LG)],
            txi.at[i], ld_tx.at[i],
        )

    for i in range(16):
        tx_load(i).start()

    barrier = pltpu.get_barrier_semaphore()
    for to in (partner, right, left):
        pl.semaphore_signal(barrier, inc=1, device_id=to, device_id_type=MESH)

    def greet(i, c):
        ii = i + 1
        to = dev(x, (y + ii // 8) % 4, (z + ii % 8) % 8, co)
        pl.semaphore_signal(barrier, inc=1, device_id=to, device_id_type=MESH)
        return c

    lax.fori_loop(0, 31, greet, 0)

    l_rx.wait()
    l_ap.wait()

    def conv(i, c):
        rows = pl.ds(pl.multiple_of(64 * i, 64), 64)
        rxs[0, rows, :] = rxi[0, rows, :].astype(F32).astype(BF16)
        rxs[1, rows, :] = rxi[1, rows, :].astype(F32).astype(BF16)
        return c

    lax.fori_loop(0, 16, conv, 0)
    own = pl.ds(pl.multiple_of(64 * g, 64), 64)
    rxa[g, 0] = rxs[0, own, :]
    rxa[g, 1] = rxs[1, own, :]
    pl.semaphore_wait(barrier, 34)

    half = pl.ds(pl.multiple_of(32 * co, 32), 32)
    step = 2 * zl - 1

    def rx_copy(i, to_y, to_z):
        gt = to_y * 4 + to_z // 2
        return rcopy(
            rxs.at[:, pl.ds(pl.multiple_of(64 * gt + 32 * co, 32), 32), :],
            rxa.at[g, :, half, :],
            rx_s.at[i], rx_r.at[g], dev(x, to_y, to_z, co),
        )

    def rx_start(i, c):
        rx_copy(i, (y + i // 3) % 4, (z + step * (1 + i % 3) + 8) % 8).start()
        return c

    def rx_start_y(i, c):
        rx_copy(12 + i, (y + 1 + i) % 4, z).start()
        return c

    lax.fori_loop(0, 12, rx_start, 0)
    lax.fori_loop(0, 3, rx_start_y, 0)

    l_sg.wait()
    signs_t = sg[...].astype(F32).T.astype(BF16)
    for i in range(4):
        enc_load(i).wait()

        def widen(j, c, i=i):
            e = pl.multiple_of(64 * i + 16 * j, 16)
            v = encb[pl.ds(e, 16)].astype(F32).reshape(256, 512)
            for b in range(4):
                encf[b, pl.ds(pl.multiple_of(e * 16, 256), 256), :] = v[:, 128 * b : 128 * b + 128]
            return c

        lax.fori_loop(0, 4, widen, 0)

    def decode(r, c):
        v = jnp.concatenate(
            [encf[b, pl.ds(r, 256, stride=16), :] for b in range(4)], axis=1
        ).astype(BF16)
        d = lax.dot_general(
            signs_t, v, (((1,), (0,)), ((), ())), preferred_element_type=F32
        )
        for b in range(4):
            part[pl.ds(b * 16 + r, 64, stride=64), :] = d[:, b * 128 : (b + 1) * 128]
        return c

    lax.fori_loop(0, 16, decode, 0)

    def prow(t, h):
        return pl.ds(pl.multiple_of(1024 * t + 512 * h, 512), 512)

    def sw_copy(i):
        zz = (1 - zl) if i < 2 else zl
        return rcopy(
            part.at[prow(2 * zz + 1 - co, i % 2), :], rb.at[i],
            sw_s.at[i], sw_r.at[i], partner,
        )

    for i in range(4):
        sw_copy(i).start()

    def ze_copy(h):
        return rcopy(zs.at[h], zb.at[h], ze_s.at[h], ze_r.at[h], mate)

    for h in range(2):
        sw_copy(h).wait_recv()
        zs[h] = part[prow(2 * (1 - zl) + co, h), :] + rb[h]
        ze_copy(h).start()

    def fw_copy(gs):
        ref = rxa.at[gs, :, half, :]
        return rcopy(ref, ref, fw_s.at[gs], fw_r.at[gs], partner)

    def fw(i, c):
        gs = (g + 1 + i) % 16
        pltpu.make_async_copy(
            rxa.at[gs, :, half, :], rxa.at[gs, :, half, :], rx_r.at[gs]
        ).wait()
        fw_copy(gs).start()
        return c

    lax.fori_loop(0, 15, fw, 0)

    def xg_copy(i, slot, h, to):
        ref = da.at[slot, pl.ds(512 * h, 512), :]
        return rcopy(ref, ref, xg_s.at[i], xg_r.at[i], to)

    for h in range(2):
        sw_copy(2 + h).wait_recv()
        ze_copy(h).wait_recv()
        tot = part[prow(tx, h), :] + rb[2 + h] + zb[h]
        da[x, pl.ds(512 * h, 512), :] = (tot * (1.0 / 1024)).astype(BF16)
        xg_copy(h, x, h, right).start()
        xg_copy(2 + h, x, h, left).start()
    xg_copy(0, xl, 0, right).wait_recv()
    xg_copy(4, xl, 0, right).start()
    xg_copy(3, xr, 1, left).wait_recv()
    xg_copy(5, xr, 1, left).start()
    xg_copy(1, xl, 1, right).wait_recv()
    xg_copy(2, xr, 0, left).wait_recv()
    xg_copy(4, x, 0, right).wait_recv()
    xg_copy(5, x, 1, left).wait_recv()

    def fw_wait(i, c):
        gs = (g + 1 + i) % 16
        oth = rxa.at[gs, :, pl.ds(pl.multiple_of(32 * (1 - co), 32), 32), :]
        pltpu.make_async_copy(oth, oth, fw_r.at[gs]).wait()
        return c

    lax.fori_loop(0, 15, fw_wait, 0)
    for i in range(16):
        tx_load(i).wait()

    def flip(k, acc):
        rows = pl.ds(pl.multiple_of(64 * k, 64), 64)
        v = jnp.concatenate([da[i, rows, :] for i in range(4)], axis=0)
        t = v.astype(F32).T
        dt[pl.ds(pl.multiple_of(128 * k, 128), 128), :] = t.astype(BF16)
        return acc + t

    total = lax.fori_loop(0, 16, flip, jnp.zeros((128, 256), F32))
    hi = total.astype(BF16)
    sh[0:128, :] = hi
    sh[128:256, :] = (total - hi.astype(F32)).astype(BF16)

    def ci_copy(i):
        return rcopy(send.at[i], ib.at[i], ci_s.at[i], ci_r.at[i], partner)

    def y_copy(i):
        d = i // 4
        to = dev(x, (y + 1 + d) % 4, z, co)
        return rcopy(ys.at[i], yb.at[i], y_s.at[i], y_r.at[i], to)

    def finish(i):
        ci_copy(i).wait_recv()
        tot = keep[i] + ib[i]

        @pl.when(i < 12)
        def _():
            ys[i] = tot.astype(BF16)
            y_copy(i).start()

        @pl.when(i >= 12)
        def _():
            keep[i] = tot

    def block(i, c):
        gt = ((y + 1 + i // 4) % 4) * 4 + i % 4
        rxv = rxa[gt, 0].astype(F32)
        apv = rxa[gt, 1].astype(F32)
        v0 = jnp.where(rxv == 0.0, apv, 0.0)
        v1 = jnp.where(rxv == 1.0, apv, 0.0)
        v2 = jnp.where(rxv == 2.0, apv, 0.0)
        zero = jnp.zeros_like(v0)
        ws = (-v0, v0 - v1, v1 - v2, v2)
        bs = (v0, v1, v2, zero)

        def rows_of(parts):
            return jnp.concatenate(
                [parts[b][16 * i : 16 * i + 16] for i in range(4) for b in range(4)], axis=0
            ).astype(BF16)

        w = rows_of(ws)
        base = jnp.dot(sh[...], rows_of(bs), preferred_element_type=F32)
        delta[...] = jnp.dot(dt[...], w, preferred_element_type=F32)
        t = txi[gt].astype(F32)
        for q in range(4):
            acc = base[32 * q : 32 * q + 32] + base[128 + 32 * q : 160 + 32 * q]
            for k in range(16):
                acc = acc + t[k : k + 1] * delta[128 * k + 32 * q : 128 * k + 32 * q + 32, :]
            to_keep = (q % 2) == co

            @pl.when(to_keep)
            def _(acc=acc, q=q):
                keep[i, q // 2] = acc

            @pl.when(jnp.logical_not(to_keep))
            def _(acc=acc, q=q):
                send[i, q // 2] = acc

        ci_copy(i).start()

        @pl.when(i > 0)
        def _():
            finish(i - 1)

        return c

    lax.fori_loop(0, 16, block, 0)
    finish(15)

    def z_copy(d):
        zt = (z + d) % 8
        return rcopy(zss.at[zt], zrb.at[d - 1], z_s.at[d - 1], z_r.at[d - 1], dev(x, y, zt, co))

    def y_wait(i, c):
        y_copy(i).wait_recv()
        return c

    lax.fori_loop(0, 12, y_wait, 0)

    def ysum(h, c):
        for q in range(2):
            tot = keep[12 + h, q]
            for d in range(3):
                tot = tot + yb[4 * d + h, q].astype(F32)
            zss[2 * h + q] = tot
        return c

    lax.fori_loop(0, 4, ysum, 0)
    for d in range(1, 8):
        z_copy(d).start()
    for d in range(1, 8):
        z_copy(d).wait_recv()
    tot = zss[z]
    for d in range(7):
        tot = tot + zrb[d]
    out_ref[...] = (tot * 0.125).T

    for i in range(4):
        sw_copy(i).wait_send()
    for h in range(2):
        ze_copy(h).wait_send()

    def drain_rx(i, c):
        rx_copy(i, y, z).wait_send()
        fw_copy((g + 1 + i) % 16).wait_send()
        return c

    lax.fori_loop(0, 15, drain_rx, 0)
    for i, (slot, h, to) in enumerate(
        ((x, 0, right), (x, 1, right), (x, 0, left), (x, 1, left), (xl, 0, right), (xr, 1, left))
    ):
        xg_copy(i, slot, h, to).wait_send()

    def drain_ci(i, c):
        ci_copy(i).wait_send()
        return c

    lax.fori_loop(0, 16, drain_ci, 0)

    def drain_y(i, c):
        y_copy(i).wait_send()
        return c

    lax.fori_loop(0, 12, drain_y, 0)
    for d in range(1, 8):
        z_copy(d).wait_send()


def on_device(encoded, signs, tx_block, rx_block, apodization):
    dma = pltpu.SemaphoreType.DMA
    hbm = pl.BlockSpec(memory_space=pl.ANY)
    return pl.pallas_call(
        kernel,
        out_shape=jax.ShapeDtypeStruct((256, 32), F32),
        in_specs=[hbm] * 5,
        out_specs=pl.BlockSpec(memory_space=pltpu.VMEM),
        scratch_shapes=[
            pltpu.VMEM((256, 16, 512), BF16),
            pltpu.VMEM((4, 4096, 128), F32),
            pltpu.VMEM((256, 64), jnp.int32),
            pltpu.VMEM((4096, 128), F32),
            pltpu.VMEM((4, 512, 128), F32),
            pltpu.VMEM((2, 512, 128), F32),
            pltpu.VMEM((2, 512, 128), F32),
            pltpu.VMEM((4, 1024, 128), BF16),
            pltpu.VMEM((2048, 256), BF16),
            pltpu.VMEM((256, 256), BF16),
            pltpu.VMEM((2, 1024, 256), jnp.int32),
            pltpu.VMEM((2, 1024, 256), BF16),
            pltpu.VMEM((16, 2, 64, 256), BF16),
            pltpu.VMEM((16, 16, 256), jnp.int32),
            pltpu.VMEM((2048, 256), F32),
            pltpu.VMEM((16, 2, 32, 256), F32),
            pltpu.VMEM((16, 2, 32, 256), F32),
            pltpu.VMEM((16, 2, 32, 256), F32),
            pltpu.VMEM((12, 2, 32, 256), BF16),
            pltpu.VMEM((12, 2, 32, 256), BF16),
            pltpu.VMEM((8, 32, 256), F32),
            pltpu.VMEM((7, 32, 256), F32),
            dma((4,)), dma((2,)), dma, dma((16,)),
            dma((15,)), dma((16,)), dma((16,)), dma((16,)),
            dma((4,)), dma((4,)), dma((2,)), dma((2,)), dma((6,)), dma((6,)),
            dma((16,)), dma((16,)), dma((12,)), dma((12,)), dma((7,)), dma((7,)),
        ],
        compiler_params=pltpu.CompilerParams(
            collective_id=0, has_side_effects=True, vmem_limit_bytes=60 * 1024 * 1024
        ),
    )(encoded, signs, tx_block, rx_block, apodization)


def solution(mesh):
    placed = (P("tx", "img", None), P(), P("tx", None), P(None, "img"), P(None, "img"))
    return jax.shard_map(
        on_device, mesh=mesh, in_specs=placed, out_specs=P("img", "tx"), check_vma=False
    )
```

time: 439 us -> 74.4 us (0.17)
  waiting for transfers between devices: 282 us -> 0 us
  local copies, waits for them, and re-layouts: 89.6 us -> 3.54 us
  Pallas kernels: 0 us -> 69.5 us
  other arithmetic: 28.7 us -> 0 us
  matrix products: 22 us -> 0 us
  between operations: 13.2 us -> 0.01 us
    all_gather x2 -> x0, waiting for transfers between devices: 246 us -> none  [the longest x1 157 us: on_device(): piece = lax.all_gather(encoded, 'tx', axis=0, tiled=True)]
    pallas_call x0 -> x1, Pallas kernels: none -> 69.5 us  [on_device(): pl.pallas_call(kernel, out_shape=jax.ShapeDtypeStruct((256, 32), F32), in...]
    select_n x1 -> x0, local copies, waits for them, and re-layouts: 46.2 us -> none  [weights_for(): jnp.where(chosen, mask_rows.T[:, None, :, None].astype(jnp.bfloat16), jnp...]
    reduce_scatter x1 -> x0, waiting for transfers between devices: 35 us -> none  [on_device(): lax.psum_scatter(image * scale, 'tx', scatter_dimension=1, tiled=True)]
    reshape x1 -> x0, local copies, waits for them, and re-layouts: 26.6 us -> none  [on_device(): lax.all_gather(decoded, 'img', axis=1, tiled=True).reshape(-1, L)]
    dot_general x2 -> x0, matrix products: 22 us -> none  [the longest x1 18.7 us: on_device(): jnp.dot(weight, lax.all_gather(decoded, 'img', axis=1, tiled=True).reshap...]
    select_n x1 -> x0, other arithmetic: 21.2 us -> none  [weights_for(): jnp.where(chosen, mask_rows.T[:, None, :, None].astype(jnp.bfloat16), jnp...]
    unnamed x10 -> x1, local copies, waits for them, and re-layouts: 16.7 us -> 1.94 us
  transfers between devices with their start and end apart: 3 -> 0, of which waited for: 3 -> 0; matrix products, arithmetic and copies ran while one was open for 17% -> 0% of each run, Pallas kernels for 0% -> 0%
where the time goes in v1:
time: 74.4 us; the launch traced here: 73.1 us
  Pallas kernels  69.5 us (93%)
  local copies, waits for them, and re-layouts  3.54 us (5%)
    pallas_call x1, Pallas kernels, on_device(): pl.pallas_call(kernel, out_shape=jax.ShapeDtypeStruct((256, 32), F32), in...  69.5 us
    unnamed x1, local copies, waits for them, and re-layouts  1.94 us
    pallas_call x1, local copies, waits for them, and re-layouts, on_device(): pl.pallas_call(kernel, out_shape=jax.ShapeDtypeStruct((256, 32), F32), in...  1.59 us

profile of v1, /device:TPU:2, one launch (start us, length us, event | category | flops | bytes accessed | tf_op | source)
XLA Modules:
  0.0 73.1 jit_solution(5578607998281181976)
XLA Ops:
  0.0 1.9 %copy.6.signs_hbm = s32[1024,64]{1,0:T(8,128)} copy(s32[1024,64]{0,1:T(8,128)} %param.6) | data formatting | bytes 524288 | tf_op args[1]
  1.9 69.5 %shard_map.55 = f32[256,32]{1,0:T(8,128)} custom-call(bf16[256,16,512]{2,1,0:T(8,128)(2,1)} %enc_hbm.1, s32[1024,64]{1,0:T(8,128)} %copy.6.signs_hbm, s32[16,16384]{1,0:T(8,128)} %tx_hbm.1, s32[1024,256]{1,0:T(8,128)} %rx_hbm.1, s32[1024,256]{1,0:T(8,128)} %apo_hbm.1), custom_call_target="tpu_custom_call" | custom-call | tf_op jit(solution)/shard_map/pallas_call | solution.py:354
  71.5 1.6 %copy.7 = f32[256,32]{0,1:T(8,128)} copy(f32[256,32]{1,0:T(8,128)} %shard_map.55) | data formatting | bytes 65536 | tf_op jit(solution)/shard_map/pallas_call | solution.py:354

commit v2 on v1

v2 whole, which is shorter than its diff:
```python
import jax
import jax.numpy as jnp
from jax import lax
from jax.experimental import pallas as pl
from jax.experimental.pallas import tpu as pltpu
from jax.sharding import PartitionSpec as P

MESH = pl.DeviceIdType.MESH
F32 = jnp.float32
BF16 = jnp.bfloat16
LG = 256
NCH = 4
CH = 1024 // NCH
LAG = 3


def kernel(
    enc_hbm, signs_hbm, tx_hbm, rx_hbm, apo_hbm, out_ref,
    encb, encf, sg, part, rb, zs, zb, zsc, zbc, da, dt, sh, rxi, rxs, rxa, txi,
    delta, keep, send, ib, ys, yb, zss, zrb,
    ld_enc, ld_rx, ld_sg, ld_tx,
    rx_s, rx_r, fw_s, fw_r, sw_s, sw_r, ze_s, ze_r, zc_s, zc_r, xg_s, xg_r,
    ci_s, ci_r, y_s, y_r, z_s, z_r,
):
    tx = lax.axis_index("tx")
    img = lax.axis_index("img")
    zl = tx // 2
    co = tx % 2
    y = img // 16
    zh = (img // 4) % 4
    x = img % 4
    z = zh * 2 + zl
    g = y * 4 + zh

    def dev(xx, yy, zz, cc):
        return {"tx": (zz % 2) * 2 + cc, "img": (yy * 4 + zz // 2) * 4 + xx}

    partner = dev(x, y, z, 1 - co)
    mate = dev(x, y, zh * 2 + (1 - zl), co)
    xr = (x + 1) % 4
    xl = (x + 3) % 4
    right = dev(xr, y, z, co)
    left = dev(xl, y, z, co)

    def rcopy(src, dst, ss, rs, to):
        return pltpu.make_async_remote_copy(
            src_ref=src, dst_ref=dst, send_sem=ss, recv_sem=rs,
            device_id=to, device_id_type=MESH,
        )

    def enc_load(i):
        return pltpu.make_async_copy(
            enc_hbm.at[pl.ds(64 * i, 64)], encb.at[pl.ds(64 * i, 64)], ld_enc.at[i]
        )

    l_rx = pltpu.make_async_copy(rx_hbm, rxi.at[0], ld_rx.at[0])
    l_ap = pltpu.make_async_copy(apo_hbm, rxi.at[1], ld_rx.at[1])
    l_sg = pltpu.make_async_copy(
        signs_hbm.at[:, pl.ds(pl.multiple_of(256 * tx, 256), 256)], sg, ld_sg
    )
    l_rx.start()
    l_ap.start()
    l_sg.start()
    for i in range(4):
        enc_load(i).start()

    def tx_load(i):
        return pltpu.make_async_copy(
            tx_hbm.at[:, pl.ds(pl.multiple_of(LG * (4 * i + x), LG), LG)],
            txi.at[i], ld_tx.at[i],
        )

    for i in range(16):
        tx_load(i).start()

    barrier = pltpu.get_barrier_semaphore()
    for to in (partner, right, left):
        pl.semaphore_signal(barrier, inc=1, device_id=to, device_id_type=MESH)

    def greet(i, c):
        ii = i + 1
        to = dev(x, (y + ii // 8) % 4, (z + ii % 8) % 8, co)
        pl.semaphore_signal(barrier, inc=1, device_id=to, device_id_type=MESH)
        return c

    lax.fori_loop(0, 31, greet, 0)

    l_sg.wait()
    signs_t = sg[...].astype(F32).astype(BF16)
    for i in range(4):
        enc_load(i).wait()

        def widen(j, c, i=i):
            e = pl.multiple_of(64 * i + 16 * j, 16)
            v = encb[pl.ds(e, 16)].astype(F32)
            for h in range(2):
                w = v[:, 8 * h : 8 * h + 8].reshape(128, 512)
                for b in range(4):
                    encf[h, b, pl.ds(pl.multiple_of(e * 8, 128), 128), :] = w[
                        :, 128 * b : 128 * b + 128
                    ]
            return c

        lax.fori_loop(0, 4, widen, 0)

    def decode(r, c):
        v = jnp.concatenate(
            [encf[r // 8, b, pl.ds(r % 8, 256, stride=8), :] for b in range(4)], axis=1
        ).astype(BF16)
        d = lax.dot_general(
            signs_t, v, (((1,), (0,)), ((), ())), preferred_element_type=F32
        )
        for b in range(4):
            part[pl.ds(b * 16 + r, 64, stride=64), :] = d[:, b * 128 : (b + 1) * 128]
        return c

    lax.fori_loop(0, 16, decode, 0)

    l_rx.wait()
    l_ap.wait()

    def conv(i, c):
        rows = pl.ds(pl.multiple_of(64 * i, 64), 64)
        rxs[0, rows, :] = rxi[0, rows, :].astype(F32).astype(BF16)
        rxs[1, rows, :] = rxi[1, rows, :].astype(F32).astype(BF16)
        return c

    lax.fori_loop(0, 16, conv, 0)
    own = pl.ds(pl.multiple_of(64 * g, 64), 64)
    rxa[g, 0] = rxs[0, own, :]
    rxa[g, 1] = rxs[1, own, :]
    pl.semaphore_wait(barrier, 34)

    def prow(t, h):
        return pl.ds(pl.multiple_of(1024 * t + CH * h, CH), CH)

    def sw_copy(i):
        zz = (1 - zl) if i < NCH else zl
        return rcopy(
            part.at[prow(2 * zz + 1 - co, i % NCH), :], rb.at[i],
            sw_s.at[i], sw_r.at[i], partner,
        )

    for i in range(2 * NCH):
        sw_copy(i).start()

    half = pl.ds(pl.multiple_of(32 * co, 32), 32)
    step = 2 * zl - 1

    def rx_copy(i, to_y, to_z):
        gt = to_y * 4 + to_z // 2
        return rcopy(
            rxs.at[:, pl.ds(pl.multiple_of(64 * gt + 32 * co, 32), 32), :],
            rxa.at[g, :, half, :],
            rx_s.at[i], rx_r.at[g], dev(x, to_y, to_z, co),
        )

    def rx_start(i, c):
        rx_copy(i, (y + i // 3) % 4, (z + step * (1 + i % 3) + 8) % 8).start()
        return c

    def rx_start_y(i, c):
        rx_copy(12 + i, (y + 1 + i) % 4, z).start()
        return c

    def ze_copy(h):
        return rcopy(zs.at[h], zb.at[h], ze_s.at[h], ze_r.at[h], mate)

    def zc_copy(h):
        return rcopy(zsc.at[h], zbc.at[h], zc_s.at[h], zc_r.at[h], mate)

    for h in range(NCH):
        sw_copy(h).wait_recv()
        v = (part[prow(2 * (1 - zl) + co, h), :] + rb[h]).reshape(CH // 8, 8, 128)
        top = jnp.maximum(jnp.max(jnp.abs(v), axis=0), 1e-30)
        q = jnp.round(v * (32767.0 / top)[None]).astype(jnp.int32)
        zs[h] = q.reshape(CH, 128).astype(jnp.int16)
        zsc[h] = top * (1.0 / 32767.0)
        ze_copy(h).start()
        zc_copy(h).start()
        if h == 0:
            lax.fori_loop(0, 12, rx_start, 0)
            lax.fori_loop(0, 3, rx_start_y, 0)

    def xg_copy(i, slot, h, to):
        ref = da.at[slot, pl.ds(CH * h, CH), :]
        return rcopy(ref, ref, xg_s.at[i], xg_r.at[i], to)

    def relay(h):
        if h % 2 == 0:
            xg_copy(h, xl, h, right).wait_recv()
            xg_copy(2 * NCH + h, xl, h, right).start()
        else:
            xg_copy(NCH + h, xr, h, left).wait_recv()
            xg_copy(2 * NCH + h, xr, h, left).start()

    for h in range(NCH):
        sw_copy(NCH + h).wait_recv()
        ze_copy(h).wait_recv()
        zc_copy(h).wait_recv()
        v = zb[h].astype(jnp.int32).astype(F32).reshape(CH // 8, 8, 128) * zbc[h][None]
        tot = part[prow(tx, h), :] + rb[NCH + h] + v.reshape(CH, 128)
        da[x, pl.ds(CH * h, CH), :] = (tot * (1.0 / 1024)).astype(BF16)
        xg_copy(h, x, h, right).start()
        xg_copy(NCH + h, x, h, left).start()
        if h > 0:
            relay(h - 1)
    relay(NCH - 1)

    def fw_copy(gs):
        ref = rxa.at[gs, :, half, :]
        return rcopy(ref, ref, fw_s.at[gs], fw_r.at[gs], partner)

    def fw(i, c):
        gs = (g + 1 + i) % 16
        pltpu.make_async_copy(
            rxa.at[gs, :, half, :], rxa.at[gs, :, half, :], rx_r.at[gs]
        ).wait()
        fw_copy(gs).start()
        return c

    lax.fori_loop(0, 15, fw, 0)

    def flip(k, acc):
        rows = pl.ds(pl.multiple_of(64 * k, 64), 64)
        v = jnp.concatenate([da[i, rows, :] for i in range(4)], axis=0)
        t = v.astype(F32).T
        dt[pl.ds(pl.multiple_of(128 * k, 128), 128), :] = t.astype(BF16)
        return acc + t

    total = jnp.zeros((128, 256), F32)
    for h in range(NCH):
        if h % 2 == 0:
            xg_copy(NCH + h, xr, h, left).wait_recv()
        else:
            xg_copy(h, xl, h, right).wait_recv()
        xg_copy(2 * NCH + h, x, h, right).wait_recv()
        total = lax.fori_loop(h * (16 // NCH), (h + 1) * (16 // NCH), flip, total)
    hi = total.astype(BF16)
    sh[0:128, :] = hi
    sh[128:256, :] = (total - hi.astype(F32)).astype(BF16)

    def fw_wait(i, c):
        gs = (g + 1 + i) % 16
        oth = rxa.at[gs, :, pl.ds(pl.multiple_of(32 * (1 - co), 32), 32), :]
        pltpu.make_async_copy(oth, oth, fw_r.at[gs]).wait()
        return c

    lax.fori_loop(0, 15, fw_wait, 0)
    for i in range(16):
        tx_load(i).wait()

    def ci_copy(i):
        return rcopy(send.at[i], ib.at[i], ci_s.at[i], ci_r.at[i], partner)

    def y_copy(i):
        to = dev(x, (y + 1 + i % 4) % 4, z, co)
        return rcopy(ys.at[i], yb.at[i], y_s.at[i], y_r.at[i], to)

    def finish(i):
        ci_copy(i).wait_recv()
        tot = keep[i] + ib[i]

        @pl.when(i % 4 < 3)
        def _():
            ys[i] = tot.astype(BF16)
            y_copy(i).start()

        @pl.when(i % 4 == 3)
        def _():
            keep[i] = tot

    def z_copy(zt):
        d = (zt - z + 8) % 8 - 1
        return rcopy(zss.at[zt], zrb.at[d], z_s.at[d], z_r.at[d], dev(x, y, zt, co))

    def z_group(n):
        for d in range(3):
            y_copy(4 * n + d).wait_recv()
        for q in range(2):
            tot = keep[4 * n + 3, q]
            for d in range(3):
                tot = tot + yb[4 * n + d, q].astype(F32)
            zt = 2 * ((zh + 1 + n) % 4) + q
            zss[zt] = tot

            @pl.when(zt != z)
            def _(zt=zt):
                z_copy(zt).start()

    def block(i, c):
        gt = ((y + 1 + i % 4) % 4) * 4 + (zh + 1 + i // 4) % 4
        rxv = rxa[gt, 0].astype(F32)
        apv = rxa[gt, 1].astype(F32)
        v0 = jnp.where(rxv == 0.0, apv, 0.0)
        v1 = jnp.where(rxv == 1.0, apv, 0.0)
        v2 = jnp.where(rxv == 2.0, apv, 0.0)
        zero = jnp.zeros_like(v0)
        ws = (-v0, v0 - v1, v1 - v2, v2)
        bs = (v0, v1, v2, zero)

        def rows_of(parts):
            return jnp.concatenate(
                [parts[b][16 * i : 16 * i + 16] for i in range(4) for b in range(4)], axis=0
            ).astype(BF16)

        w = rows_of(ws)
        base = jnp.dot(sh[...], rows_of(bs), preferred_element_type=F32)
        delta[...] = jnp.dot(dt[...], w, preferred_element_type=F32)
        t = txi[gt].astype(F32)
        for q in range(4):
            acc = base[32 * q : 32 * q + 32] + base[128 + 32 * q : 160 + 32 * q]
            for k in range(16):
                acc = acc + t[k : k + 1] * delta[128 * k + 32 * q : 128 * k + 32 * q + 32, :]
            to_keep = (q % 2) == co

            @pl.when(to_keep)
            def _(acc=acc, q=q):
                keep[i, q // 2] = acc

            @pl.when(jnp.logical_not(to_keep))
            def _(acc=acc, q=q):
                send[i, q // 2] = acc

        ci_copy(i).start()

        @pl.when(i >= LAG)
        def _():
            finish(i - LAG)

        @pl.when(jnp.logical_and(i - LAG >= 7, (i - LAG) % 4 == 3))
        def _():
            z_group((i - LAG - 7) // 4)

        return c

    lax.fori_loop(0, 16, block, 0)
    for i in range(16 - LAG, 16):
        finish(i)
    z_group(2)
    z_group(3)
    for d in range(1, 8):
        z_copy((z + d) % 8).wait_recv()
    tot = zss[z]
    for d in range(7):
        tot = tot + zrb[d]
    out_ref[...] = tot * 0.125

    for i in range(2 * NCH):
        sw_copy(i).wait_send()
    for h in range(NCH):
        ze_copy(h).wait_send()
        zc_copy(h).wait_send()

    def drain_rx(i, c):
        rx_copy(i, y, z).wait_send()
        fw_copy((g + 1 + i) % 16).wait_send()
        return c

    lax.fori_loop(0, 15, drain_rx, 0)
    for i in range(3 * NCH):
        xg_copy(i, x, i % NCH, right).wait_send()

    def drain_ci(i, c):
        ci_copy(i).wait_send()

        @pl.when(i % 4 < 3)
        def _():
            y_copy(i).wait_send()

        return c

    lax.fori_loop(0, 16, drain_ci, 0)
    for d in range(1, 8):
        z_copy((z + d) % 8).wait_send()


def on_device(encoded, signs, tx_block, rx_block, apodization):
    dma = pltpu.SemaphoreType.DMA
    hbm = pl.BlockSpec(memory_space=pl.ANY)
    return pl.pallas_call(
        kernel,
        out_shape=jax.ShapeDtypeStruct((32, 256), F32),
        in_specs=[hbm] * 5,
        out_specs=pl.BlockSpec(memory_space=pltpu.VMEM),
        scratch_shapes=[
            pltpu.VMEM((256, 16, 512), BF16),
            pltpu.VMEM((2, 4, 2048, 128), F32),
            pltpu.VMEM((64, 256), jnp.int32),
            pltpu.VMEM((4096, 128), F32),
            pltpu.VMEM((2 * NCH, CH, 128), F32),
            pltpu.VMEM((NCH, CH, 128), jnp.int16),
            pltpu.VMEM((NCH, CH, 128), jnp.int16),
            pltpu.VMEM((NCH, 8, 128), F32),
            pltpu.VMEM((NCH, 8, 128), F32),
            pltpu.VMEM((4, 1024, 128), BF16),
            pltpu.VMEM((2048, 256), BF16),
            pltpu.VMEM((256, 256), BF16),
            pltpu.VMEM((2, 1024, 256), jnp.int32),
            pltpu.VMEM((2, 1024, 256), BF16),
            pltpu.VMEM((16, 2, 64, 256), BF16),
            pltpu.VMEM((16, 16, 256), jnp.int32),
            pltpu.VMEM((2048, 256), F32),
            pltpu.VMEM((16, 2, 32, 256), F32),
            pltpu.VMEM((16, 2, 32, 256), F32),
            pltpu.VMEM((16, 2, 32, 256), F32),
            pltpu.VMEM((16, 2, 32, 256), BF16),
            pltpu.VMEM((16, 2, 32, 256), BF16),
            pltpu.VMEM((8, 32, 256), F32),
            pltpu.VMEM((7, 32, 256), F32),
            dma((4,)), dma((2,)), dma, dma((16,)),
            dma((15,)), dma((16,)), dma((16,)), dma((16,)),
            dma((2 * NCH,)), dma((2 * NCH,)), dma((NCH,)), dma((NCH,)), dma((NCH,)), dma((NCH,)),
            dma((3 * NCH,)), dma((3 * NCH,)),
            dma((16,)), dma((16,)), dma((16,)), dma((16,)), dma((7,)), dma((7,)),
        ],
        compiler_params=pltpu.CompilerParams(
            collective_id=0, has_side_effects=True, vmem_limit_bytes=60 * 1024 * 1024
        ),
    )(encoded, signs.T, tx_block, rx_block, apodization).T


def solution(mesh):
    placed = (P("tx", "img", None), P(), P("tx", None), P(None, "img"), P(None, "img"))
    return jax.shard_map(
        on_device, mesh=mesh, in_specs=placed, out_specs=P("img", "tx"), check_vma=False
    )
```

time: 74.4 us -> 58 us (0.78)
  Pallas kernels: 69.5 us -> 55.5 us
  local copies, waits for them, and re-layouts: 3.54 us -> 1.38 us
    pallas_call x1, Pallas kernels: 69.5 us -> 55.5 us  [on_device(): pl.pallas_call(kernel, out_shape=jax.ShapeDtypeStruct((32, 256), F32), in...]
    pallas_call x1 -> x0, local copies, waits for them, and re-layouts: 1.59 us -> none  [on_device(): pl.pallas_call(kernel, out_shape=jax.ShapeDtypeStruct((256, 32), F32), in...]
where the time goes in v2:
time: 58 us; the launch traced here: 56.9 us
  Pallas kernels  55.5 us (96%)
  local copies, waits for them, and re-layouts  1.38 us (2%)
    pallas_call x1, Pallas kernels, on_device(): pl.pallas_call(kernel, out_shape=jax.ShapeDtypeStruct((32, 256), F32), in...  55.5 us
    unnamed x1, local copies, waits for them, and re-layouts  1.38 us

profile of v2, /device:TPU:2, one launch (start us, length us, event | category | flops | bytes accessed | tf_op | source)
XLA Modules:
  0.0 56.9 jit_solution(9967074286974705845)
XLA Ops:
  0.0 55.5 %shard_map.55 = f32[32,256]{1,0:T(8,128)} custom-call(bf16[256,16,512]{2,1,0:T(8,128)(2,1)} %enc_hbm.1, s32[64,1024]{1,0:T(8,128)} %bitcast.2, s32[16,16384]{1,0:T(8,128)} %tx_hbm.1, s32[1024,256]{1,0:T(8,128)} %rx_hbm.1, s32[1024,256]{1,0:T(8,128)} %apo_hbm.1), custom_call_target="tpu_custom_call" | custom-call | tf_op jit(solution)/shard_map/pallas_call | solution.py:381
  55.5 1.4 %copy.7 = f32[256,32]{0,1:T(8,128)} copy(f32[256,32]{0,1:T(8,128)} %bitcast.3) | data formatting | bytes 65536

commit v3 on v2

--- a/solution.py
+++ b/solution.py
@@ -12,15 +12,25 @@
 NCH = 4
 CH = 1024 // NCH
 LAG = 3
+AHEAD = 4
+
+
+def packed(table):
+    word = sum(v << (2 * i) for i, v in enumerate(table))
+    return word - (1 << 32) if word >> 31 else word
+
+
+ORDER_Z = packed((1, 1, 1, 3, 3, 3, 0, 1, 2, 2, 2, 0, 0, 3, 2, 0))
+ORDER_Y = packed((2, 1, 3, 2, 1, 3, 2, 0, 2, 1, 3, 1, 3, 0, 0, 0))
 
 
 def kernel(
     enc_hbm, signs_hbm, tx_hbm, rx_hbm, apo_hbm, out_ref,
-    encb, encf, sg, part, rb, zs, zb, zsc, zbc, da, dt, sh, rxi, rxs, rxa, txi,
-    delta, keep, send, ib, ys, yb, zss, zrb,
+    encb, encf, sg, part, rb, zs, zb, zsc, zbc, da, dt, rxi, rxs, rxa, txi,
+    delta, keep, send, ib, ys, yb, zss, zrb, zown,
     ld_enc, ld_rx, ld_sg, ld_tx,
     rx_s, rx_r, fw_s, fw_r, sw_s, sw_r, ze_s, ze_r, zc_s, zc_r, xg_s, xg_r,
-    ci_s, ci_r, y_s, y_r, z_s, z_r,
+    ci_s, ci_r, y_s, y_r, z_s, z_r, ready,
 ):
     tx = lax.axis_index("tx")
     img = lax.axis_index("img")
@@ -41,6 +51,7 @@
     xl = (x + 3) % 4
     right = dev(xr, y, z, co)
     left = dev(xl, y, z, co)
+    across = dev((x + 2) % 4, y, z, co)
 
     def rcopy(src, dst, ss, rs, to):
         return pltpu.make_async_remote_copy(
@@ -58,11 +69,11 @@
     l_sg = pltpu.make_async_copy(
         signs_hbm.at[:, pl.ds(pl.multiple_of(256 * tx, 256), 256)], sg, ld_sg
     )
-    l_rx.start()
-    l_ap.start()
     l_sg.start()
     for i in range(4):
         enc_load(i).start()
+    l_rx.start()
+    l_ap.start()
 
     def tx_load(i):
         return pltpu.make_async_copy(
@@ -74,16 +85,15 @@
         tx_load(i).start()
 
     barrier = pltpu.get_barrier_semaphore()
-    for to in (partner, right, left):
+    for to in (partner, right, left, across):
         pl.semaphore_signal(barrier, inc=1, device_id=to, device_id_type=MESH)
 
-    def greet(i, c):
-        ii = i + 1
-        to = dev(x, (y + ii // 8) % 4, (z + ii % 8) % 8, co)
+    for d in range(1, 4):
+        to = dev(x, (y + d) % 4, z, co)
         pl.semaphore_signal(barrier, inc=1, device_id=to, device_id_type=MESH)
-        return c
-
-    lax.fori_loop(0, 31, greet, 0)
+    for d in range(1, 8):
+        to = dev(x, y, (z + d) % 8, co)
+        pl.semaphore_signal(barrier, inc=1, device_id=to, device_id_type=MESH)
 
     l_sg.wait()
     signs_t = sg[...].astype(F32).astype(BF16)
@@ -114,7 +124,7 @@
             part[pl.ds(b * 16 + r, 64, stride=64), :] = d[:, b * 128 : (b + 1) * 128]
         return c
 
-    lax.fori_loop(0, 16, decode, 0)
+    lax.fori_loop(0, 16, decode, 0, unroll=4)
 
     l_rx.wait()
     l_ap.wait()
@@ -129,7 +139,10 @@
     own = pl.ds(pl.multiple_of(64 * g, 64), 64)
     rxa[g, 0] = rxs[0, own, :]
     rxa[g, 1] = rxs[1, own, :]
-    pl.semaphore_wait(barrier, 34)
+    pl.semaphore_wait(barrier, 14)
+    for d in range(1, 4):
+        to = dev(x, (y + d) % 4, z, co)
+        pl.semaphore_signal(ready, inc=1, device_id=to, device_id_type=MESH)
 
     def prow(t, h):
         return pl.ds(pl.multiple_of(1024 * t + CH * h, CH), CH)
@@ -156,12 +169,19 @@
         )
 
     def rx_start(i, c):
-        rx_copy(i, (y + i // 3) % 4, (z + step * (1 + i % 3) + 8) % 8).start()
+        d = jnp.where(i < 8, 1 + i % 2, 3)
+        yy = jnp.where(i < 8, i // 2, i - 8)
+        rx_copy(i, (y + yy + 1) % 4, (z + step * d + 8) % 8).start()
         return c
 
     def rx_start_y(i, c):
         rx_copy(12 + i, (y + 1 + i) % 4, z).start()
         return c
+
+    pl.semaphore_wait(ready, 3)
+    lax.fori_loop(0, 8, rx_start, 0)
+    lax.fori_loop(0, 3, rx_start_y, 0)
+    lax.fori_loop(8, 12, rx_start, 0)
 
     def ze_copy(h):
         return rcopy(zs.at[h], zb.at[h], ze_s.at[h], ze_r.at[h], mate)
@@ -178,16 +198,15 @@
         zsc[h] = top * (1.0 / 32767.0)
         ze_copy(h).start()
         zc_copy(h).start()
-        if h == 0:
-            lax.fori_loop(0, 12, rx_start, 0)
-            lax.fori_loop(0, 3, rx_start_y, 0)
 
     def xg_copy(i, slot, h, to):
         ref = da.at[slot, pl.ds(CH * h, CH), :]
         return rcopy(ref, ref, xg_s.at[i], xg_r.at[i], to)
 
     def relay(h):
-        if h % 2 == 0:
+        if h == NCH - 1:
+            return
+        if h == 0:
             xg_copy(h, xl, h, right).wait_recv()
             xg_copy(2 * NCH + h, xl, h, right).start()
         else:
@@ -201,115 +220,141 @@
         v = zb[h].astype(jnp.int32).astype(F32).reshape(CH // 8, 8, 128) * zbc[h][None]
         tot = part[prow(tx, h), :] + rb[NCH + h] + v.reshape(CH, 128)
         da[x, pl.ds(CH * h, CH), :] = (tot * (1.0 / 1024)).astype(BF16)
+        if h == NCH - 1:
+            xg_copy(2 * NCH + h, x, h, across).start()
         xg_copy(h, x, h, right).start()
         xg_copy(NCH + h, x, h, left).start()
         if h > 0:
             relay(h - 1)
     relay(NCH - 1)
 
+    def dz_of(i):
+        return (ORDER_Z >> (2 * i)) & 3
+
+    def dy_of(i):
+        return (ORDER_Y >> (2 * i)) & 3
+
+    def gt_of(i):
+        return ((y + dy_of(i)) % 4) * 4 + (zh + dz_of(i)) % 4
+
     def fw_copy(gs):
         ref = rxa.at[gs, :, half, :]
         return rcopy(ref, ref, fw_s.at[gs], fw_r.at[gs], partner)
 
-    def fw(i, c):
-        gs = (g + 1 + i) % 16
+    def fw(i):
+        gs = gt_of(i)
         pltpu.make_async_copy(
             rxa.at[gs, :, half, :], rxa.at[gs, :, half, :], rx_r.at[gs]
         ).wait()
         fw_copy(gs).start()
-        return c
-
-    lax.fori_loop(0, 15, fw, 0)
+
+    def fw_first(i, c):
+        fw(i)
+        return c
+
+    lax.fori_loop(0, AHEAD, fw_first, 0)
 
     def flip(k, acc):
         rows = pl.ds(pl.multiple_of(64 * k, 64), 64)
-        v = jnp.concatenate([da[i, rows, :] for i in range(4)], axis=0)
-        t = v.astype(F32).T
-        dt[pl.ds(pl.multiple_of(128 * k, 128), 128), :] = t.astype(BF16)
-        return acc + t
-
-    total = jnp.zeros((128, 256), F32)
+        v = jnp.concatenate([da[i, rows, :] for i in range(4)], axis=0).astype(F32)
+        dt[pl.ds(pl.multiple_of(128 * k, 128), 128), :] = v.T.astype(BF16)
+        return acc + v
+
+    total = jnp.zeros((256, 128), F32)
     for h in range(NCH):
-        if h % 2 == 0:
+        if h == 0 or h == NCH - 1:
             xg_copy(NCH + h, xr, h, left).wait_recv()
-        else:
+        if h > 0:
             xg_copy(h, xl, h, right).wait_recv()
         xg_copy(2 * NCH + h, x, h, right).wait_recv()
         total = lax.fori_loop(h * (16 // NCH), (h + 1) * (16 // NCH), flip, total)
-    hi = total.astype(BF16)
-    sh[0:128, :] = hi
-    sh[128:256, :] = (total - hi.astype(F32)).astype(BF16)
-
-    def fw_wait(i, c):
-        gs = (g + 1 + i) % 16
+    pieces = []
+    for i in range(4):
+        d0, d1, d2 = (total[64 * i + 16 * b : 64 * i + 16 * b + 16] for b in range(3))
+        pieces += [-(d0 + d1), -d1, jnp.zeros_like(d2), d2]
+    base_t = jnp.concatenate(pieces, axis=0).T
+    hi = base_t.astype(BF16)
+    dt[2048:2176, :] = hi
+    dt[2176:2304, :] = (base_t - hi.astype(F32)).astype(BF16)
+
+    def fw_wait(i):
+        gs = gt_of(i)
         oth = rxa.at[gs, :, pl.ds(pl.multiple_of(32 * (1 - co), 32), 32), :]
         pltpu.make_async_copy(oth, oth, fw_r.at[gs]).wait()
-        return c
-
-    lax.fori_loop(0, 15, fw_wait, 0)
+
     for i in range(16):
         tx_load(i).wait()
 
     def ci_copy(i):
         return rcopy(send.at[i], ib.at[i], ci_s.at[i], ci_r.at[i], partner)
 
-    def y_copy(i):
-        to = dev(x, (y + 1 + i % 4) % 4, z, co)
-        return rcopy(ys.at[i], yb.at[i], y_s.at[i], y_r.at[i], to)
-
-    def finish(i):
-        ci_copy(i).wait_recv()
-        tot = keep[i] + ib[i]
-
-        @pl.when(i % 4 < 3)
-        def _():
-            ys[i] = tot.astype(BF16)
-            y_copy(i).start()
-
-        @pl.when(i % 4 == 3)
-        def _():
-            keep[i] = tot
+    def slot_of(i):
+        d = dy_of(i)
+        return dz_of(i) * 3 + jnp.where(d == 2, 0, jnp.where(d == 1, 1, 2))
+
+    def y_copy(m, d):
+        to = dev(x, (y + d) % 4, z, co)
+        return rcopy(ys.at[m], yb.at[m], y_s.at[m], y_r.at[m], to)
 
     def z_copy(zt):
         d = (zt - z + 8) % 8 - 1
         return rcopy(zss.at[zt], zrb.at[d], z_s.at[d], z_r.at[d], dev(x, y, zt, co))
 
-    def z_group(n):
-        for d in range(3):
-            y_copy(4 * n + d).wait_recv()
-        for q in range(2):
-            tot = keep[4 * n + 3, q]
+    def finish(i):
+        ci_copy(i).wait_recv()
+
+        @pl.when(dy_of(i) != 0)
+        def _():
+            m = slot_of(i)
+            ys[m] = (keep[i] + ib[i]).astype(BF16)
+            y_copy(m, dy_of(i)).start()
+
+        @pl.when(dy_of(i) == 0)
+        def _():
+            n = dz_of(i)
             for d in range(3):
-                tot = tot + yb[4 * n + d, q].astype(F32)
-            zt = 2 * ((zh + 1 + n) % 4) + q
-            zss[zt] = tot
-
-            @pl.when(zt != z)
-            def _(zt=zt):
-                z_copy(zt).start()
+                y_copy(3 * n + d, 1).wait_recv()
+            for q in range(2):
+                tot = keep[i, q] + ib[i, q]
+                for d in range(3):
+                    tot = tot + yb[3 * n + d, q].astype(F32)
+                zt = 2 * ((zh + n) % 4) + q
+                zss[zt] = tot.astype(BF16)
+
+                @pl.when(zt != z)
+                def _(zt=zt):
+                    z_copy(zt).start()
+
+                @pl.when(zt == z)
+                def _(tot=tot):
+                    zown[...] = tot
 
     def block(i, c):
-        gt = ((y + 1 + i % 4) % 4) * 4 + (zh + 1 + i // 4) % 4
+        gt = gt_of(i)
+
+        @pl.when(i + AHEAD < 15)
+        def _():
+            fw(i + AHEAD)
+
+        @pl.when(i < 15)
+        def _():
+            fw_wait(i)
+
         rxv = rxa[gt, 0].astype(F32)
         apv = rxa[gt, 1].astype(F32)
         v0 = jnp.where(rxv == 0.0, apv, 0.0)
         v1 = jnp.where(rxv == 1.0, apv, 0.0)
         v2 = jnp.where(rxv == 2.0, apv, 0.0)
-        zero = jnp.zeros_like(v0)
         ws = (-v0, v0 - v1, v1 - v2, v2)
-        bs = (v0, v1, v2, zero)
-
-        def rows_of(parts):
-            return jnp.concatenate(
-                [parts[b][16 * i : 16 * i + 16] for i in range(4) for b in range(4)], axis=0
-            ).astype(BF16)
-
-        w = rows_of(ws)
-        base = jnp.dot(sh[...], rows_of(bs), preferred_element_type=F32)
+        w = jnp.concatenate(
+            [ws[b][16 * i4 : 16 * i4 + 16] for i4 in range(4) for b in range(4)], axis=0
+        ).astype(BF16)
         delta[...] = jnp.dot(dt[...], w, preferred_element_type=F32)
         t = txi[gt].astype(F32)
         for q in range(4):
-            acc = base[32 * q : 32 * q + 32] + base[128 + 32 * q : 160 + 32 * q]
+            acc = (
+                delta[2048 + 32 * q : 2080 + 32 * q, :] + delta[2176 + 32 * q : 2208 + 32 * q, :]
+            )
             for k in range(16):
                 acc = acc + t[k : k + 1] * delta[128 * k + 32 * q : 128 * k + 32 * q + 32, :]
             to_keep = (q % 2) == co
@@ -328,23 +373,11 @@
         def _():
             finish(i - LAG)
 
-        @pl.when(jnp.logical_and(i - LAG >= 7, (i - LAG) % 4 == 3))
-        def _():
-            z_group((i - LAG - 7) // 4)
-
         return c
 
     lax.fori_loop(0, 16, block, 0)
     for i in range(16 - LAG, 16):
         finish(i)
-    z_group(2)
-    z_group(3)
-    for d in range(1, 8):
-        z_copy((z + d) % 8).wait_recv()
-    tot = zss[z]
-    for d in range(7):
-        tot = tot + zrb[d]
-    out_ref[...] = tot * 0.125
 
     for i in range(2 * NCH):
         sw_copy(i).wait_send()
@@ -354,7 +387,7 @@
 
     def drain_rx(i, c):
         rx_copy(i, y, z).wait_send()
-        fw_copy((g + 1 + i) % 16).wait_send()
+        fw_copy(gt_of(i)).wait_send()
         return c
 
     lax.fori_loop(0, 15, drain_rx, 0)
@@ -363,16 +396,24 @@
 
     def drain_ci(i, c):
         ci_copy(i).wait_send()
-
-        @pl.when(i % 4 < 3)
-        def _():
-            y_copy(i).wait_send()
-
         return c
 
     lax.fori_loop(0, 16, drain_ci, 0)
+
+    def drain_y(i, c):
+        y_copy(i, 1).wait_send()
+        return c
+
+    lax.fori_loop(0, 12, drain_y, 0)
     for d in range(1, 8):
         z_copy((z + d) % 8).wait_send()
+
+    for d in range(1, 8):
+        z_copy((z + d) % 8).wait_recv()
+    tot = zown[...]
+    for d in range(7):
+        tot = tot + zrb[d].astype(F32)
+    out_ref[...] = tot * 0.125
 
 
 def on_device(encoded, signs, tx_block, rx_block, apodization):
@@ -394,25 +435,25 @@
             pltpu.VMEM((NCH, 8, 128), F32),
             pltpu.VMEM((NCH, 8, 128), F32),
             pltpu.VMEM((4, 1024, 128), BF16),
-            pltpu.VMEM((2048, 256), BF16),
-            pltpu.VMEM((256, 256), BF16),
+            pltpu.VMEM((2304, 256), BF16),
             pltpu.VMEM((2, 1024, 256), jnp.int32),
             pltpu.VMEM((2, 1024, 256), BF16),
             pltpu.VMEM((16, 2, 64, 256), BF16),
             pltpu.VMEM((16, 16, 256), jnp.int32),
-            pltpu.VMEM((2048, 256), F32),
+            pltpu.VMEM((2304, 256), F32),
             pltpu.VMEM((16, 2, 32, 256), F32),
             pltpu.VMEM((16, 2, 32, 256), F32),
             pltpu.VMEM((16, 2, 32, 256), F32),
-            pltpu.VMEM((16, 2, 32, 256), BF16),
-            pltpu.VMEM((16, 2, 32, 256), BF16),
-            pltpu.VMEM((8, 32, 256), F32),
-            pltpu.VMEM((7, 32, 256), F32),
+            pltpu.VMEM((12, 2, 32, 256), BF16),
+            pltpu.VMEM((12, 2, 32, 256), BF16),
+            pltpu.VMEM((8, 32, 256), BF16),
+            pltpu.VMEM((7, 32, 256), BF16),
+            pltpu.VMEM((32, 256), F32),
             dma((4,)), dma((2,)), dma, dma((16,)),
             dma((15,)), dma((16,)), dma((16,)), dma((16,)),
             dma((2 * NCH,)), dma((2 * NCH,)), dma((NCH,)), dma((NCH,)), dma((NCH,)), dma((NCH,)),
             dma((3 * NCH,)), dma((3 * NCH,)),
-            dma((16,)), dma((16,)), dma((16,)), dma((16,)), dma((7,)), dma((7,)),
+            dma((16,)), dma((16,)), dma((12,)), dma((12,)), dma((7,)), dma((7,)), pltpu.SemaphoreType.REGULAR,
         ],
         compiler_params=pltpu.CompilerParams(
             collective_id=0, has_side_effects=True, vmem_limit_bytes=60 * 1024 * 1024

time: 58 us -> 56.3 us (0.971); the launches traced: 56.9 us -> 56.1 us
  Pallas kernels: 55.5 us -> 54.8 us
    pallas_call x1, Pallas kernels: 55.5 us -> 54.8 us  [on_device(): pl.pallas_call(kernel, out_shape=jax.ShapeDtypeStruct((32, 256), F32), in...]
where the time goes in v3:
time: 56.3 us; the launch traced here: 56.1 us
  Pallas kernels  54.8 us (97%)
  local copies, waits for them, and re-layouts  1.38 us (2%)
    pallas_call x1, Pallas kernels, on_device(): pl.pallas_call(kernel, out_shape=jax.ShapeDtypeStruct((32, 256), F32), in...  54.8 us
    unnamed x1, local copies, waits for them, and re-layouts  1.38 us

profile of v3, /device:TPU:2, one launch (start us, length us, event | category | flops | bytes accessed | tf_op | source)
XLA Modules:
  0.0 56.1 jit_solution(6155193141397062870)
XLA Ops:
  0.0 54.8 %shard_map.55 = f32[32,256]{1,0:T(8,128)} custom-call(bf16[256,16,512]{2,1,0:T(8,128)(2,1)} %enc_hbm.1, s32[64,1024]{1,0:T(8,128)} %bitcast.2, s32[16,16384]{1,0:T(8,128)} %tx_hbm.1, s32[1024,256]{1,0:T(8,128)} %rx_hbm.1, s32[1024,256]{1,0:T(8,128)} %apo_hbm.1), custom_call_target="tpu_custom_call" | custom-call | tf_op jit(solution)/shard_map/pallas_call | solution.py:422
  54.8 1.4 %copy.7 = f32[256,32]{0,1:T(8,128)} copy(f32[256,32]{0,1:T(8,128)} %bitcast.3) | data formatting | bytes 65536

commit v4 on v3

--- a/solution.py
+++ b/solution.py
@@ -20,8 +20,8 @@
     return word - (1 << 32) if word >> 31 else word
 
 
-ORDER_Z = packed((1, 1, 1, 3, 3, 3, 0, 1, 2, 2, 2, 0, 0, 3, 2, 0))
-ORDER_Y = packed((2, 1, 3, 2, 1, 3, 2, 0, 2, 1, 3, 1, 3, 0, 0, 0))
+ORDER_Z = packed((1, 1, 1, 0, 2, 2, 2, 1, 3, 3, 3, 2, 0, 0, 3, 0))
+ORDER_Y = packed((2, 1, 3, 2, 2, 1, 3, 0, 2, 1, 3, 0, 1, 3, 0, 0))
 
 
 def kernel(

time: 56.3 us -> 54.7 us (0.972)
  Pallas kernels: 54.8 us -> 53.2 us
    pallas_call x1, Pallas kernels: 54.8 us -> 53.2 us  [on_device(): pl.pallas_call(kernel, out_shape=jax.ShapeDtypeStruct((32, 256), F32), in...]
where the time goes in v4:
time: 54.7 us; the launch traced here: 54.6 us
  Pallas kernels  53.2 us (97%)
  local copies, waits for them, and re-layouts  1.38 us (3%)
    pallas_call x1, Pallas kernels, on_device(): pl.pallas_call(kernel, out_shape=jax.ShapeDtypeStruct((32, 256), F32), in...  53.2 us
    unnamed x1, local copies, waits for them, and re-layouts  1.38 us

profile of v4, /device:TPU:2, one launch (start us, length us, event | category | flops | bytes accessed | tf_op | source)
XLA Modules:
  0.0 54.6 jit_solution(4892799054967373938)
XLA Ops:
  0.0 53.2 %shard_map.55 = f32[32,256]{1,0:T(8,128)} custom-call(bf16[256,16,512]{2,1,0:T(8,128)(2,1)} %enc_hbm.1, s32[64,1024]{1,0:T(8,128)} %bitcast.2, s32[16,16384]{1,0:T(8,128)} %tx_hbm.1, s32[1024,256]{1,0:T(8,128)} %rx_hbm.1, s32[1024,256]{1,0:T(8,128)} %apo_hbm.1), custom_call_target="tpu_custom_call" | custom-call | tf_op jit(solution)/shard_map/pallas_call | solution.py:422
  53.2 1.4 %copy.7 = f32[256,32]{0,1:T(8,128)} copy(f32[256,32]{0,1:T(8,128)} %bitcast.3) | data formatting | bytes 65536

commit v5 on v4

--- a/solution.py
+++ b/solution.py
@@ -20,8 +20,8 @@
     return word - (1 << 32) if word >> 31 else word
 
 
-ORDER_Z = packed((1, 1, 1, 0, 2, 2, 2, 1, 3, 3, 3, 2, 0, 0, 3, 0))
-ORDER_Y = packed((2, 1, 3, 2, 2, 1, 3, 0, 2, 1, 3, 0, 1, 3, 0, 0))
+ORDER_Z = packed((1,1,1,2,2,2,3,3,3,1,0,0,0,2,3,0))
+ORDER_Y = packed((2,1,3,2,1,3,2,1,3,0,2,1,3,0,0,0))
 
 
 def kernel(
@@ -126,19 +126,6 @@
 
     lax.fori_loop(0, 16, decode, 0, unroll=4)
 
-    l_rx.wait()
-    l_ap.wait()
-
-    def conv(i, c):
-        rows = pl.ds(pl.multiple_of(64 * i, 64), 64)
-        rxs[0, rows, :] = rxi[0, rows, :].astype(F32).astype(BF16)
-        rxs[1, rows, :] = rxi[1, rows, :].astype(F32).astype(BF16)
-        return c
-
-    lax.fori_loop(0, 16, conv, 0)
-    own = pl.ds(pl.multiple_of(64 * g, 64), 64)
-    rxa[g, 0] = rxs[0, own, :]
-    rxa[g, 1] = rxs[1, own, :]
     pl.semaphore_wait(barrier, 14)
     for d in range(1, 4):
         to = dev(x, (y + d) % 4, z, co)
@@ -157,6 +144,19 @@
     for i in range(2 * NCH):
         sw_copy(i).start()
 
+    l_rx.wait()
+    l_ap.wait()
+
+    def conv(i, c):
+        rows = pl.ds(pl.multiple_of(64 * i, 64), 64)
+        rxs[0, rows, :] = rxi[0, rows, :].astype(F32).astype(BF16)
+        rxs[1, rows, :] = rxi[1, rows, :].astype(F32).astype(BF16)
+        return c
+
+    lax.fori_loop(0, 16, conv, 0)
+    own = pl.ds(pl.multiple_of(64 * g, 64), 64)
+    rxa[g, 0] = rxs[0, own, :]
+    rxa[g, 1] = rxs[1, own, :]
     half = pl.ds(pl.multiple_of(32 * co, 32), 32)
     step = 2 * zl - 1
 
@@ -178,10 +178,6 @@
         rx_copy(12 + i, (y + 1 + i) % 4, z).start()
         return c
 
-    pl.semaphore_wait(ready, 3)
-    lax.fori_loop(0, 8, rx_start, 0)
-    lax.fori_loop(0, 3, rx_start_y, 0)
-    lax.fori_loop(8, 12, rx_start, 0)
 
     def ze_copy(h):
         return rcopy(zs.at[h], zb.at[h], ze_s.at[h], ze_r.at[h], mate)
@@ -198,6 +194,11 @@
         zsc[h] = top * (1.0 / 32767.0)
         ze_copy(h).start()
         zc_copy(h).start()
+        if h == 0:
+            pl.semaphore_wait(ready, 3)
+            lax.fori_loop(0, 8, rx_start, 0)
+            lax.fori_loop(0, 3, rx_start_y, 0)
+            lax.fori_loop(8, 12, rx_start, 0)
 
     def xg_copy(i, slot, h, to):
         ref = da.at[slot, pl.ds(CH * h, CH), :]

time: 54.7 us -> 52.8 us (0.965)
  Pallas kernels: 53.2 us -> 51.1 us
    pallas_call x1, Pallas kernels: 53.2 us -> 51.1 us  [on_device(): pl.pallas_call(kernel, out_shape=jax.ShapeDtypeStruct((32, 256), F32), in...]
where the time goes in v5:
time: 52.8 us; the launch traced here: 52.5 us
  Pallas kernels  51.1 us (97%)
  local copies, waits for them, and re-layouts  1.38 us (3%)
    pallas_call x1, Pallas kernels, on_device(): pl.pallas_call(kernel, out_shape=jax.ShapeDtypeStruct((32, 256), F32), in...  51.1 us
    unnamed x1, local copies, waits for them, and re-layouts  1.38 us

profile of v5, /device:TPU:2, one launch (start us, length us, event | category | flops | bytes accessed | tf_op | source)
XLA Modules:
  0.0 52.5 jit_solution(11742554702314358624)
XLA Ops:
  0.0 51.1 %shard_map.55 = f32[32,256]{1,0:T(8,128)} custom-call(bf16[256,16,512]{2,1,0:T(8,128)(2,1)} %enc_hbm.1, s32[64,1024]{1,0:T(8,128)} %bitcast.2, s32[16,16384]{1,0:T(8,128)} %tx_hbm.1, s32[1024,256]{1,0:T(8,128)} %rx_hbm.1, s32[1024,256]{1,0:T(8,128)} %apo_hbm.1), custom_call_target="tpu_custom_call" | custom-call | tf_op jit(solution)/shard_map/pallas_call | solution.py:423
  51.1 1.4 %copy.7 = f32[256,32]{0,1:T(8,128)} copy(f32[256,32]{0,1:T(8,128)} %bitcast.3) | data formatting | bytes 65536

commit v6 on v5

--- a/solution.py
+++ b/solution.py
@@ -124,7 +124,7 @@
             part[pl.ds(b * 16 + r, 64, stride=64), :] = d[:, b * 128 : (b + 1) * 128]
         return c
 
-    lax.fori_loop(0, 16, decode, 0, unroll=4)
+    lax.fori_loop(0, 16, decode, 0, unroll=8)
 
     pl.semaphore_wait(barrier, 14)
     for d in range(1, 4):

time: 52.8 us -> 52.6 us (level)
  no operation moved by 1% of the time
where the time goes in v6:
time: 52.6 us; the launch traced here: 52.1 us
  Pallas kernels  50.7 us (96%)
  local copies, waits for them, and re-layouts  1.38 us (3%)
    pallas_call x1, Pallas kernels, on_device(): pl.pallas_call(kernel, out_shape=jax.ShapeDtypeStruct((32, 256), F32), in...  50.7 us
    unnamed x1, local copies, waits for them, and re-layouts  1.38 us

profile of v6, /device:TPU:2, one launch (start us, length us, event | category | flops | bytes accessed | tf_op | source)
XLA Modules:
  0.0 52.1 jit_solution(11373490393754426006)
XLA Ops:
  0.0 50.7 %shard_map.55 = f32[32,256]{1,0:T(8,128)} custom-call(bf16[256,16,512]{2,1,0:T(8,128)(2,1)} %enc_hbm.1, s32[64,1024]{1,0:T(8,128)} %bitcast.2, s32[16,16384]{1,0:T(8,128)} %tx_hbm.1, s32[1024,256]{1,0:T(8,128)} %rx_hbm.1, s32[1024,256]{1,0:T(8,128)} %apo_hbm.1), custom_call_target="tpu_custom_call" | custom-call | tf_op jit(solution)/shard_map/pallas_call | solution.py:423
  50.7 1.4 %copy.7 = f32[256,32]{0,1:T(8,128)} copy(f32[256,32]{0,1:T(8,128)} %bitcast.3) | data formatting | bytes 65536
